TPU v7x, 32 devices: a whole 2x2x4 slice. The times are simulated.
32 devices in a mesh: leaf: 8 (over z, x), vec: 4 (over y, core).
Axes of the slice: x: 2, y: 2, z: 4, core: 2. Of those that a mesh axis runs over, the one named last changes fastest.
Arguments:
- vectors: float32 [32, 65536], P('vec', 'leaf'), may hold values from -15 to 15
- coords: float32 [3, 65536], P(None, 'leaf'), may hold values from 0 to 64, as said below
- leaf_basis: float32 [32, 65536], P(None, 'leaf'), may hold values from -0.375 to 0.375
- node_ops: float32 [496, 32, 128], P('leaf'), may hold values from -0.75 to 0.75
- top_ops: float32 [2, 32, 192], replicated, may hold values from -0.75 to 0.75
- near_target: int32 [1280], P('leaf'), may hold values from 0 to 255, as said below
- near_source: int32 [1280], P('leaf'), may hold values from 0 to 255, as said below
- near_count: int32 [8], P('leaf'), may hold values from 64 to 160, as said below
Outputs:
- product: float32 [32, 65536], P('vec', 'leaf')
- gram_matrix: float32 [32, 32], P(None, 'vec')
Inputs may be any that keep to these rules, and one draw needn't show every extreme that they name: `near_target`: slots of one index of leaf name target leaves of that index only; each aligned block of 32 slots of an index names each of its leaves once; in the first run every leaf is paired with itself, and in the second run the first leaf of each index is paired with the leaf just below it and the last leaf with the leaf just above it, where those exist. `near_source`: A source leaf lies within 4 leaves of its target leaf; no pair repeats within one index of leaf. The first near_count[d] slots of index d are live, the rest are padding; some index fills all 160 slots. `coords`: point k lies in the box of its leaf l = k // 256: first coordinate from 0.25 l to 0.25 (l + 1), the other two from 0 to 1.
All inputs are finite; a program needn't handle non-finite values.
Results may differ from a plain program's by a relative error of at most 0.0003.
Values sent between devices are 32-bit elements; how exact they have to be, the bound alone decides.
A program may use at most 64 MiB of HBM per device.

v0:
```python
import jax
import jax.numpy as jnp
import numpy as np
from jax import lax
from jax.sharding import PartitionSpec as P

PTS = 256
NEAR_REACH = 4
EXACT_ARITHMETIC = lax.Precision.HIGHEST
SIGNAL = 0.1
NUGGET = 0.5
LENGTH = 0.35
EVEN_OFFSETS = (-2, 2, 3)
ODD_OFFSETS = (-3, -2, 2)


def padded_2(block, sides, width):
    for axis, dim in sides:
        count = lax.axis_size(axis)
        forward = [(i, i + 1) for i in range(count - 1)]
        backward = [(target, source) for source, target in forward]
        low = lax.ppermute(
            lax.slice_in_dim(block, block.shape[dim] - width, None, axis=dim), axis, forward
        )
        high = lax.ppermute(lax.slice_in_dim(block, 0, width, axis=dim), axis, backward)
        block = jnp.concatenate([low, block, high], axis=dim)
    return block


def matern(target_pts, source_pts):
    pair_separation = jnp.zeros(
        (target_pts.shape[1], target_pts.shape[2], source_pts.shape[2]), jnp.float32
    )
    for axis_id in range(3):
        spacing = target_pts[axis_id][:, :, None] - source_pts[axis_id][:, None, :]
        pair_separation = pair_separation + spacing * spacing
    scaled = jnp.sqrt(3.0 * pair_separation) / LENGTH
    return SIGNAL * (1.0 + scaled) * jnp.exp(-scaled)


def take_rows(padded, count_nodes, pad_width):
    parity_ids = np.arange(count_nodes) % 2
    gathered = []
    for slot_index in range(3):
        shift_by = np.where(parity_ids == 0, EVEN_OFFSETS[slot_index], ODD_OFFSETS[slot_index])
        gathered.append(padded[np.arange(count_nodes) + shift_by + pad_width])
    return jnp.stack(gathered, axis=1)


def couple_level(padded, operators, count_nodes, pad_width, rank_size):
    sources = take_rows(padded, count_nodes, pad_width)
    blocks = operators[:, :, : 3 * rank_size].reshape(count_nodes, rank_size, 3, rank_size)
    return jnp.einsum("navr,nras->nvs", sources, blocks, precision=EXACT_ARITHMETIC)


def raise_level(incoming_coefficients, operators, rank_size):
    moved = jnp.einsum(
        "nvr,nrs->nvs",
        incoming_coefficients,
        operators[:, :, 3 * rank_size :],
        precision=EXACT_ARITHMETIC,
    )
    return moved[0::2] + moved[1::2]


def lower_level(field_in, operators, rank_size):
    spread = jnp.repeat(field_in, 2, axis=0)
    return jnp.einsum(
        "nvs,nrs->nvr", spread, operators[:, :, 3 * rank_size :], precision=EXACT_ARITHMETIC
    )


def through(incoming_coefficients, operators, position, rank_size):
    return jnp.einsum(
        "...r,rs->...s",
        incoming_coefficients,
        operators[:, position * rank_size : (position + 1) * rank_size],
        precision=EXACT_ARITHMETIC,
    )


def couple_top(partners, operators, parity, rank_size):
    far_left, near_left, near_right, far_right = partners
    outer = jnp.where(
        parity == 0,
        through(far_right, operators, 3, rank_size),
        through(far_left, operators, 0, rank_size),
    )
    return (
        through(near_left, operators, 1, rank_size)
        + through(near_right, operators, 2, rank_size)
        + outer
    )


def raise_pair(left_coef, right_coef, operators, rank_size):
    return through(left_coef, operators, 4, rank_size) + through(
        right_coef, operators, 5, rank_size
    )


def lower_top(field_in, operators, parity, rank_size):
    even_part = jnp.einsum(
        "...s,rs->...r",
        field_in,
        operators[:, 4 * rank_size : 5 * rank_size],
        precision=EXACT_ARITHMETIC,
    )
    odd_part = jnp.einsum(
        "...s,rs->...r",
        field_in,
        operators[:, 5 * rank_size : 6 * rank_size],
        precision=EXACT_ARITHMETIC,
    )
    return jnp.where(parity == 0, even_part, odd_part)


def near_field(window, local_coords, targets, sources, weights, pair_block):
    columns = window.shape[0] - 3
    leaves_dev = local_coords.shape[1]
    step_count = targets.shape[0] // pair_block

    def add_block(accumulated_sum, portion):
        target_ids, source_ids, live_mask = portion
        source_rows = jnp.take(window, source_ids, axis=1)
        target_pts = jnp.take(local_coords, target_ids, axis=1)
        kernel = matern(target_pts, source_rows[columns:])
        contribution = jnp.einsum(
            "vbs,bts->bvt", source_rows[:columns], kernel, precision=EXACT_ARITHMETIC
        )
        selection_mask = (target_ids[:, None] == jnp.arange(leaves_dev)[None, :]).astype(
            jnp.float32
        ) * live_mask[:, None]
        return (
            accumulated_sum
            + jnp.einsum("qs,qhg->hsg", selection_mask, contribution, precision=EXACT_ARITHMETIC),
            None,
        )

    initial = jnp.zeros((columns, leaves_dev, window.shape[2]), jnp.float32)
    portions = (
        targets.reshape(step_count, pair_block),
        sources.reshape(step_count, pair_block),
        weights.reshape(step_count, pair_block),
    )
    accumulated_sum, unused = lax.scan(add_block, initial, portions)
    return accumulated_sum.reshape(columns, leaves_dev * window.shape[2])


def on_device(vectors, coords, leaf_basis, node_ops, top_ops, near_target, near_source, near_count):
    rank_size = leaf_basis.shape[0]
    columns_dev = vectors.shape[0]
    points_dev = vectors.shape[1]
    leaves_dev = points_dev // PTS
    device = lax.axis_index("leaf")
    vec_index = lax.axis_index("vec")
    vec_count = lax.axis_size("vec")
    leaf_count = lax.axis_size("leaf")
    all_columns = lax.all_gather(vectors, "vec", axis=0, tiled=True)
    base_leaf = device * leaves_dev
    slot_ids = jnp.arange(near_target.shape[0], dtype=jnp.int32)
    live_all = (slot_ids < near_count[0]).astype(jnp.float32)
    target_all = near_target - base_leaf
    source_all = near_source - base_leaf + NEAR_REACH
    local_coords = coords.reshape(3, leaves_dev, PTS)
    stacked = jnp.concatenate([all_columns, coords], axis=0)
    window = padded_2(stacked, (("leaf", 1),), NEAR_REACH * PTS)
    window = window.reshape(all_columns.shape[0] + 3, leaves_dev + 2 * NEAR_REACH, PTS)
    share_count = near_target.shape[0] // vec_count
    slot_grid = slot_ids.reshape(share_count, vec_count)
    picked = lax.dynamic_slice_in_dim(slot_grid, vec_index, 1, 1)[:, 0]
    partial_sum = near_field(
        window,
        local_coords,
        target_all[picked],
        source_all[picked],
        live_all[picked],
        share_count // (leaves_dev // vec_count),
    )
    near_part = lax.psum_scatter(partial_sum, "vec", scatter_dimension=0, tiled=True)
    leaf_basis_matrix = leaf_basis.reshape(rank_size, leaves_dev, PTS)
    current = jnp.einsum(
        "vlp,rlp->lvr",
        vectors.reshape(columns_dev, leaves_dev, PTS),
        leaf_basis_matrix,
        precision=EXACT_ARITHMETIC,
    )
    level_ops = []
    level_fields = []
    offset_node = 0
    nodes_here = leaves_dev
    while nodes_here >= 2:
        ops_here = node_ops[offset_node : offset_node + nodes_here]
        rim_width = min(3, nodes_here)
        padded = padded_2(current, (("leaf", 0),), rim_width)
        level_fields.append(couple_level(padded, ops_here, nodes_here, rim_width, rank_size))
        level_ops.append(ops_here)
        current = raise_level(current, ops_here, rank_size)
        offset_node += nodes_here
        nodes_here //= 2
    top_levels = top_ops.shape[0]
    top_fields = []
    all_roots = lax.all_gather(current, "leaf", axis=0, tiled=True)
    for height in range(top_levels):
        padded_top = jnp.pad(all_roots, ((3, 3), (0, 0), (0, 0)))
        node_id = device // (1 << height)
        near_rows = lax.dynamic_slice_in_dim(padded_top, node_id, 7, 0)
        partners = (near_rows[0], near_rows[1], near_rows[5], near_rows[6])
        top_fields.append(couple_top(partners, top_ops[height], node_id % 2, rank_size))
        if height + 1 < top_levels:
            all_roots = raise_pair(all_roots[0::2], all_roots[1::2], top_ops[height], rank_size)
    downward = top_fields[top_levels - 1]
    for height in range(top_levels - 2, -1, -1):
        parity = device // (1 << height) % 2
        downward = top_fields[height] + lower_top(downward, top_ops[height], parity, rank_size)
    downward = downward[None]
    for index_level in range(len(level_fields) - 1, -1, -1):
        downward = level_fields[index_level] + lower_level(
            downward, level_ops[index_level], rank_size
        )
    far_part = jnp.einsum(
        "lvr,rlp->vlp", downward, leaf_basis_matrix, precision=EXACT_ARITHMETIC
    ).reshape(columns_dev, points_dev)
    product = near_part + far_part + NUGGET * vectors
    gram_part = jnp.einsum("ip,jp->ij", all_columns, product, precision=EXACT_ARITHMETIC)
    gram_matrix = lax.psum(gram_part, "leaf") / (leaf_count * points_dev)
    return (product, gram_matrix)


def solution(mesh):
    return jax.shard_map(
        on_device,
        mesh=mesh,
        in_specs=(
            P("vec", "leaf"),
            P(None, "leaf"),
            P(None, "leaf"),
            P("leaf", None, None),
            P(),
            P("leaf"),
            P("leaf"),
            P("leaf"),
        ),
        out_specs=(P("vec", "leaf"), P(None, "vec")),
        check_vma=False,
    )
```

profile of v0, /device:TPU:0, one launch (start us, length us, event | category | flops | bytes accessed | tf_op | source)
XLA Modules:
  0.0 216.0 jit_solution(17568019953974837203)
XLA Ops:
  7.2 2.3 %fusion.55 = f32[32,8,32]{2,1,0:T(8,128)S(1)} fusion(f32[8,32,256]{2,0,1:T(8,128)} %bitcast.178, f32[4,32,8,256]{3,2,1,0:T(8,128)} %bitcast.175), kind=kOutput, calls=%fused_computation.110 | convolution fusion | flops 25165824 | bytes 1343488 | tf_op jit(solution)/shard_map/vlp,rlp->lvr/dot_general | solution.py:182
  11.4 4.9 %collective-permute-start.10 = (f32[2,8,32]{2,1,0:T(8,128)S(1)}, f32[2,8,32]{2,1,0:T(8,128)S(1)}, u32[]{:S(2)}, u32[]{:S(2)}) collective-permute-start(f32[2,8,32]{2,1,0:T(8,128)S(1)} %slice_add_fusion.3), channel_id=1, source_target_pairs={{0,4},{4,8},{8,12},{12,16},{16,20},{20,24},{24,28},{1,5},{5,9},{9,... | collective-permute-start | bytes 6152 | tf_op jit(solution)/shard_map/ppermute | solution.py:22
  18.3 5.1 %collective-permute-start.8 = (f32[3,8,32]{2,1,0:T(8,128)}, f32[3,8,32]{2,1,0:T(8,128)}, u32[]{:S(2)}, u32[]{:S(2)}) collective-permute-start(f32[3,8,32]{2,1,0:T(8,128)} %get-tuple-element.113), channel_id=1, source_target_pairs={{0,4},{4,8},{8,12},{12,16},{16,20},{20,24},{24,28},{1,5},{5,9},{9,... | collective-permute-start | bytes 9224 | tf_op jit(solution)/shard_map/ppermute | solution.py:22
  24.0 4.4 %collective-permute-start.6 = (f32[3,8,32]{2,1,0:T(8,128)}, f32[3,8,32]{2,1,0:T(8,128)}, u32[]{:S(2)}, u32[]{:S(2)}) collective-permute-start(f32[3,8,32]{2,1,0:T(8,128)} %get-tuple-element.111), channel_id=1, source_target_pairs={{0,4},{4,8},{8,12},{12,16},{16,20},{20,24},{24,28},{1,5},{5,9},{9,... | collective-permute-start | bytes 9224 | tf_op jit(solution)/shard_map/ppermute | solution.py:22
  29.9 31.5 %all_gather.7 = f32[8,8,32]{2,1,0:T(8,128)S(1)} all-gather(f32[1,8,32]{2,1,0:T(8,128)S(1)} %slice_add_fusion.4), channel_id=1, replica_groups=mesh['leaf'=8,'vec'=4] {'leaf'}, dimensions={0}, use_global_device_ids=true | all-gather | bytes 9216 | tf_op jit(solution)/shard_map/all_gather | solution.py:203
  74.0 1.7 reshape.157
  78.4 1.6 collective-permute-start.4
  84.9 4.6 %collective-permute-start = (f32[35,1024]{1,0:T(8,128)S(1)}, f32[35,1024]{1,0:T(8,128)S(1)}, u32[]{:S(2)}, u32[]{:S(2)}) collective-permute-start(f32[35,1024]{1,0:T(8,128)S(1)} %get-tuple-element.103), channel_id=1, source_target_pairs={{0,4},{4,8},{8,12},{12,16},{16,20},{20,24},{24,28},{1,5},{5,9},{9,... | collective-permute-start | bytes 430088 | tf_op jit(solution)/shard_map/ppermute | solution.py:22
  92.9 5.2 %collective-permute-start.2 = (f32[3,8,32]{2,1,0:T(8,128)}, f32[3,8,32]{2,1,0:T(8,128)S(1)}, u32[]{:S(2)}, u32[]{:S(2)}) collective-permute-start(f32[3,8,32]{2,1,0:T(8,128)} %get-tuple-element.105), channel_id=1, source_target_pairs={{0,4},{4,8},{8,12},{12,16},{16,20},{20,24},{24,28},{1,5},{5,9},{9,... | collective-permute-start | bytes 9224 | tf_op jit(solution)/shard_map/ppermute | solution.py:22
  100.1 1.7 copy.66
  101.8 53.4 %while.11 = (s32[]{:T(128)}, f32[32,32,256]{2,1,0:T(8,128)S(1)}, s32[8,5]{1,0:T(8,128)S(1)}, f32[35,40,256]{2,0,1:T(8,128)}, s32[8,5]{1,0:T(8,128)S(1)}, /*index...) while((s32[]{:T(128)}, f32[32,32,256]{2,1,0:T(8,128)S(1)}, ...), condition=%wide.region_1.2_spmd.clone, body=%wide.region_0.1_spmd.clone.sunk | while | flops 146720672 | bytes 3547571 | solution.py:146
  101.8 2.0 gather_fusion
  104.7 2.4 %fusion.205 = f32[5,32,256]{2,1,0:T(8,128)S(1)} fusion(f32[5,256]{1,0:T(8,128)S(1)} %bitcast.189, f32[5,256]{1,0:T(8,128)S(1)} %bitcast.192, f32[5,256]{1,0:T(8,128)S(1)} %bitcast.190, f32[5,256]{1,0:T(8,128)S(1)} %bitcast.193, f32[5,256]{1,0:T(8,128)S(1)} %bitcast.191, f32[5,256]{1,0:T(8,128)S(1)} %bitcast.194, ...), kind=kOutput, calls=%fused_computation.22.clone.1 | convolution fusion | flops 130416640 | bytes 376832 | tf_op jit(solution)/shard_map/while/body/eval_jaxpr/vbs,bts->bvt/dot_general | solution.py:128
  108.5 2.0 gather_fusion
  111.4 2.4 %fusion.205 = f32[5,32,256]{2,1,0:T(8,128)S(1)} fusion(f32[5,256]{1,0:T(8,128)S(1)} %bitcast.189, f32[5,256]{1,0:T(8,128)S(1)} %bitcast.192, f32[5,256]{1,0:T(8,128)S(1)} %bitcast.190, f32[5,256]{1,0:T(8,128)S(1)} %bitcast.193, f32[5,256]{1,0:T(8,128)S(1)} %bitcast.191, f32[5,256]{1,0:T(8,128)S(1)} %bitcast.194, ...), kind=kOutput, calls=%fused_computation.22.clone.1 | convolution fusion | flops 130416640 | bytes 376832 | tf_op jit(solution)/shard_map/while/body/eval_jaxpr/vbs,bts->bvt/dot_general | solution.py:128
  115.2 2.0 gather_fusion
  118.0 2.4 %fusion.205 = f32[5,32,256]{2,1,0:T(8,128)S(1)} fusion(f32[5,256]{1,0:T(8,128)S(1)} %bitcast.189, f32[5,256]{1,0:T(8,128)S(1)} %bitcast.192, f32[5,256]{1,0:T(8,128)S(1)} %bitcast.190, f32[5,256]{1,0:T(8,128)S(1)} %bitcast.193, f32[5,256]{1,0:T(8,128)S(1)} %bitcast.191, f32[5,256]{1,0:T(8,128)S(1)} %bitcast.194, ...), kind=kOutput, calls=%fused_computation.22.clone.1 | convolution fusion | flops 130416640 | bytes 376832 | tf_op jit(solution)/shard_map/while/body/eval_jaxpr/vbs,bts->bvt/dot_general | solution.py:128
  121.8 2.0 gather_fusion
  124.7 2.4 %fusion.205 = f32[5,32,256]{2,1,0:T(8,128)S(1)} fusion(f32[5,256]{1,0:T(8,128)S(1)} %bitcast.189, f32[5,256]{1,0:T(8,128)S(1)} %bitcast.192, f32[5,256]{1,0:T(8,128)S(1)} %bitcast.190, f32[5,256]{1,0:T(8,128)S(1)} %bitcast.193, f32[5,256]{1,0:T(8,128)S(1)} %bitcast.191, f32[5,256]{1,0:T(8,128)S(1)} %bitcast.194, ...), kind=kOutput, calls=%fused_computation.22.clone.1 | convolution fusion | flops 130416640 | bytes 376832 | tf_op jit(solution)/shard_map/while/body/eval_jaxpr/vbs,bts->bvt/dot_general | solution.py:128
  128.5 2.0 gather_fusion
  131.4 2.4 %fusion.205 = f32[5,32,256]{2,1,0:T(8,128)S(1)} fusion(f32[5,256]{1,0:T(8,128)S(1)} %bitcast.189, f32[5,256]{1,0:T(8,128)S(1)} %bitcast.192, f32[5,256]{1,0:T(8,128)S(1)} %bitcast.190, f32[5,256]{1,0:T(8,128)S(1)} %bitcast.193, f32[5,256]{1,0:T(8,128)S(1)} %bitcast.191, f32[5,256]{1,0:T(8,128)S(1)} %bitcast.194, ...), kind=kOutput, calls=%fused_computation.22.clone.1 | convolution fusion | flops 130416640 | bytes 376832 | tf_op jit(solution)/shard_map/while/body/eval_jaxpr/vbs,bts->bvt/dot_general | solution.py:128
  135.2 2.0 gather_fusion
  138.1 2.4 %fusion.205 = f32[5,32,256]{2,1,0:T(8,128)S(1)} fusion(f32[5,256]{1,0:T(8,128)S(1)} %bitcast.189, f32[5,256]{1,0:T(8,128)S(1)} %bitcast.192, f32[5,256]{1,0:T(8,128)S(1)} %bitcast.190, f32[5,256]{1,0:T(8,128)S(1)} %bitcast.193, f32[5,256]{1,0:T(8,128)S(1)} %bitcast.191, f32[5,256]{1,0:T(8,128)S(1)} %bitcast.194, ...), kind=kOutput, calls=%fused_computation.22.clone.1 | convolution fusion | flops 130416640 | bytes 376832 | tf_op jit(solution)/shard_map/while/body/eval_jaxpr/vbs,bts->bvt/dot_general | solution.py:128
  141.9 2.0 gather_fusion
  144.7 2.4 %fusion.205 = f32[5,32,256]{2,1,0:T(8,128)S(1)} fusion(f32[5,256]{1,0:T(8,128)S(1)} %bitcast.189, f32[5,256]{1,0:T(8,128)S(1)} %bitcast.192, f32[5,256]{1,0:T(8,128)S(1)} %bitcast.190, f32[5,256]{1,0:T(8,128)S(1)} %bitcast.193, f32[5,256]{1,0:T(8,128)S(1)} %bitcast.191, f32[5,256]{1,0:T(8,128)S(1)} %bitcast.194, ...), kind=kOutput, calls=%fused_computation.22.clone.1 | convolution fusion | flops 130416640 | bytes 376832 | tf_op jit(solution)/shard_map/while/body/eval_jaxpr/vbs,bts->bvt/dot_general | solution.py:128
  148.6 2.0 gather_fusion
  151.4 2.4 %fusion.205 = f32[5,32,256]{2,1,0:T(8,128)S(1)} fusion(f32[5,256]{1,0:T(8,128)S(1)} %bitcast.189, f32[5,256]{1,0:T(8,128)S(1)} %bitcast.192, f32[5,256]{1,0:T(8,128)S(1)} %bitcast.190, f32[5,256]{1,0:T(8,128)S(1)} %bitcast.193, f32[5,256]{1,0:T(8,128)S(1)} %bitcast.191, f32[5,256]{1,0:T(8,128)S(1)} %bitcast.194, ...), kind=kOutput, calls=%fused_computation.22.clone.1 | convolution fusion | flops 130416640 | bytes 376832 | tf_op jit(solution)/shard_map/while/body/eval_jaxpr/vbs,bts->bvt/dot_general | solution.py:128
  155.2 1.6 copy.82
  172.9 1.8 convolution_bitcast_fusion.2
  174.8 3.2 %fusion.46 = f32[32,8,32]{2,1,0:T(8,128)S(1)} fusion(f32[32,32,3,32]{3,2,1,0:T(4,128)S(1)} %copy-done.1, f32[32,1,8,32]{3,2,0,1:T(8,128)S(1)} %bitcast.181, f32[32,1,8,32]{3,2,0,1:T(8,128)S(1)} %bitcast.180, f32[32,1,8,32]{3,2,0,1:T(8,128)} %bitcast.182), kind=kOutput, calls=%fused_computation.89 | convolution fusion | flops 9486336 | bytes 524288 | tf_op jit(solution)/shard_map/navr,nras->nvs/dot_general | solution.py:53
  182.2 3.1 %reduce-scatter.2.cloned.1.call-done = f32[8,8192]{1,0:T(8,128)} async-done(((f32[32,8192]{1,0:T(8,128)}), f32[8,8192]{1,0:T(8,128)}) %reduce-scatter.2.cloned.1.call-update) | async-done | bytes 262160 | tf_op jit(solution)/shard_map/reduce_scatter | solution.py:180
  187.2 21.4 %psum.7 = f32[32,8]{0,1:T(8,128)S(1)} all-reduce(f32[32,8]{0,1:T(8,128)S(1)} %convolution_bitcast_fusion.5), channel_id=1, replica_groups=mesh['leaf'=8,'vec'=4] {'leaf'}, use_global_device_ids=true, to_apply=%region_3.4 | all-reduce | flops 256 | bytes 2048 | tf_op jit(solution)/shard_map/psum | solution.py:226
  (317 shorter events, 70.3 us)
Async XLA Ops:
  7.2 76.3 %all-gather.2.cloned.1.call-start = ((), (), s32[]{:S(2)}) async-start(), calls=%async_computation.1 | async-start | bytes 1310720 | tf_op jit(solution)/shard_map/all_gather | solution.py:159
  9.5 51.9 %copy-start.11 = (f32[2,32,192]{2,1,0:T(8,128)S(1)}, f32[2,32,192]{2,1,0:T(8,128)}, u32[]{:S(2)}) copy-start(f32[2,32,192]{2,1,0:T(8,128)} %param.44) | copy-start | bytes 147460
  9.6 53.6 %copy-start.27 = (s32[4]{0:T(128)S(1)}, s32[4]{0:T(128)}, u32[]{:S(2)}) copy-start(s32[4]{0:T(128)} %constant.214) | copy-start | bytes 52
  9.6 54.2 %copy-start.26 = (s32[8]{0:T(128)S(1)}, s32[8]{0:T(128)}, u32[]{:S(2)}) copy-start(s32[8]{0:T(128)} %constant.211) | copy-start | bytes 100
  9.6 54.8 %copy-start.25 = (s32[16]{0:T(128)S(1)}, s32[16]{0:T(128)}, u32[]{:S(2)}) copy-start(s32[16]{0:T(128)} %constant.208) | copy-start | bytes 196
  9.6 55.4 %copy-start.24 = (s32[32]{0:T(128)S(1)}, s32[32]{0:T(128)}, u32[]{:S(2)}) copy-start(s32[32]{0:T(128)} %constant.205) | copy-start | bytes 388
  10.3 56.1 %copy-start.23 = (s32[2]{0:T(128)S(1)}, s32[2]{0:T(128)}, u32[]{:S(2)}) copy-start(s32[2]{0:T(128)} %constant.217) | copy-start | bytes 28
  10.3 56.1 %copy-start.21 = (s32[4]{0:T(128)S(1)}, s32[4]{0:T(128)}, u32[]{:S(2)}) copy-start(s32[4]{0:T(128)} %constant.215) | copy-start | bytes 52
  10.3 56.1 %copy-start.22 = (s32[4]{0:T(128)S(1)}, s32[4]{0:T(128)}, u32[]{:S(2)}) copy-start(s32[4]{0:T(128)} %constant.216) | copy-start | bytes 52
  10.3 56.7 %copy-start.19 = (s32[8]{0:T(128)S(1)}, s32[8]{0:T(128)}, u32[]{:S(2)}) copy-start(s32[8]{0:T(128)} %constant.212) | copy-start | bytes 100
  10.3 56.7 %copy-start.20 = (s32[8]{0:T(128)S(1)}, s32[8]{0:T(128)}, u32[]{:S(2)}) copy-start(s32[8]{0:T(128)} %constant.213) | copy-start | bytes 100
  10.3 57.3 %copy-start.17 = (s32[16]{0:T(128)S(1)}, s32[16]{0:T(128)}, u32[]{:S(2)}) copy-start(s32[16]{0:T(128)} %constant.209) | copy-start | bytes 196
  10.3 57.3 %copy-start.18 = (s32[16]{0:T(128)S(1)}, s32[16]{0:T(128)}, u32[]{:S(2)}) copy-start(s32[16]{0:T(128)} %constant.210) | copy-start | bytes 196
  10.4 57.9 %copy-start.15 = (s32[32]{0:T(128)S(1)}, s32[32]{0:T(128)}, u32[]{:S(2)}) copy-start(s32[32]{0:T(128)} %constant.206) | copy-start | bytes 388
  10.4 57.9 %copy-start.16 = (s32[32]{0:T(128)S(1)}, s32[32]{0:T(128)}, u32[]{:S(2)}) copy-start(s32[32]{0:T(128)} %constant.207) | copy-start | bytes 388
  10.4 58.5 %copy-start.13 = (s32[160]{0:T(256)S(1)}, s32[160]{0:T(256)}, u32[]{:S(2)}) copy-start(s32[160]{0:T(256)} %param.46) | copy-start | bytes 1924
  10.4 58.5 %copy-start.14 = (s32[160]{0:T(256)S(1)}, s32[160]{0:T(256)}, u32[]{:S(2)}) copy-start(s32[160]{0:T(256)} %param.45) | copy-start | bytes 1924
  11.4 67.0 %collective-permute-start.10 = (f32[2,8,32]{2,1,0:T(8,128)S(1)}, f32[2,8,32]{2,1,0:T(8,128)S(1)}, u32[]{:S(2)}, u32[]{:S(2)}) collective-permute-start(f32[2,8,32]{2,1,0:T(8,128)S(1)} %slice_add_fusion.3), channel_id=1, source_target_pairs={{0,4},{4,8},{8,12},{12,16},{16,20},{20,24},{24,28},{1,5},{5,9},{9,... | collective-permute-start | bytes 6152 | tf_op jit(solution)/shard_map/ppermute | solution.py:22
  16.3 63.7 %collective-permute-start.11 = (f32[2,8,32]{2,1,0:T(8,128)S(1)}, f32[2,8,32]{2,1,0:T(8,128)S(1)}, u32[]{:S(2)}, u32[]{:S(2)}) collective-permute-start(f32[2,8,32]{2,1,0:T(8,128)S(1)} %slice_add_fusion.3), channel_id=1, source_target_pairs={{4,0},{8,4},{12,8},{16,12},{20,16},{24,20},{28,24},{5,1},{9,5},{13... | collective-permute-start | bytes 6152 | tf_op jit(solution)/shard_map/ppermute | solution.py:25
  17.6 167.6 %reduce-scatter.2.cloned.1.call-start = ((), (), s32[]{:S(2)}) async-start(), calls=%async_computation.2 | async-start | bytes 1310720 | tf_op jit(solution)/shard_map/reduce_scatter | solution.py:180
  18.3 138.5 %collective-permute-start.8 = (f32[3,8,32]{2,1,0:T(8,128)}, f32[3,8,32]{2,1,0:T(8,128)}, u32[]{:S(2)}, u32[]{:S(2)}) collective-permute-start(f32[3,8,32]{2,1,0:T(8,128)} %get-tuple-element.113), channel_id=1, source_target_pairs={{0,4},{4,8},{8,12},{12,16},{16,20},{20,24},{24,28},{1,5},{5,9},{9,... | collective-permute-start | bytes 9224 | tf_op jit(solution)/shard_map/ppermute | solution.py:22
  24.0 60.9 %collective-permute-start.6 = (f32[3,8,32]{2,1,0:T(8,128)}, f32[3,8,32]{2,1,0:T(8,128)}, u32[]{:S(2)}, u32[]{:S(2)}) collective-permute-start(f32[3,8,32]{2,1,0:T(8,128)} %get-tuple-element.111), channel_id=1, source_target_pairs={{0,4},{4,8},{8,12},{12,16},{16,20},{20,24},{24,28},{1,5},{5,9},{9,... | collective-permute-start | bytes 9224 | tf_op jit(solution)/shard_map/ppermute | solution.py:22
  28.4 61.1 %collective-permute-start.7 = (f32[3,8,32]{2,1,0:T(8,128)}, f32[3,8,32]{2,1,0:T(8,128)}, u32[]{:S(2)}, u32[]{:S(2)}) collective-permute-start(f32[3,8,32]{2,1,0:T(8,128)} %get-tuple-element.112), channel_id=1, source_target_pairs={{4,0},{8,4},{12,8},{16,12},{20,16},{24,20},{28,24},{5,1},{9,5},{13... | collective-permute-start | bytes 9224 | tf_op jit(solution)/shard_map/ppermute | solution.py:25
  78.4 13.2 %collective-permute-start.4 = (f32[3,8,32]{2,1,0:T(8,128)}, f32[3,8,32]{2,1,0:T(8,128)S(1)}, u32[]{:S(2)}, u32[]{:S(2)}) collective-permute-start(f32[3,8,32]{2,1,0:T(8,128)} %get-tuple-element.107), channel_id=1, source_target_pairs={{0,4},{4,8},{8,12},{12,16},{16,20},{20,24},{24,28},{1,5},{5,9},{9,... | collective-permute-start | bytes 9224 | tf_op jit(solution)/shard_map/ppermute | solution.py:22
  80.0 12.9 %collective-permute-start.5 = (f32[3,8,32]{2,1,0:T(8,128)}, f32[3,8,32]{2,1,0:T(8,128)S(1)}, u32[]{:S(2)}, u32[]{:S(2)}) collective-permute-start(f32[3,8,32]{2,1,0:T(8,128)} %get-tuple-element.108), channel_id=1, source_target_pairs={{4,0},{8,4},{12,8},{16,12},{20,16},{24,20},{28,24},{5,1},{9,5},{13... | collective-permute-start | bytes 9224 | tf_op jit(solution)/shard_map/ppermute | solution.py:25
  84.9 13.1 %collective-permute-start = (f32[35,1024]{1,0:T(8,128)S(1)}, f32[35,1024]{1,0:T(8,128)S(1)}, u32[]{:S(2)}, u32[]{:S(2)}) collective-permute-start(f32[35,1024]{1,0:T(8,128)S(1)} %get-tuple-element.103), channel_id=1, source_target_pairs={{0,4},{4,8},{8,12},{12,16},{16,20},{20,24},{24,28},{1,5},{5,9},{9,... | collective-permute-start | bytes 430088 | tf_op jit(solution)/shard_map/ppermute | solution.py:22
  89.5 9.9 %collective-permute-start.1 = (f32[35,1024]{1,0:T(8,128)S(1)}, f32[35,1024]{1,0:T(8,128)S(1)}, u32[]{:S(2)}, u32[]{:S(2)}) collective-permute-start(f32[35,1024]{1,0:T(8,128)S(1)} %get-tuple-element.104), channel_id=1, source_target_pairs={{4,0},{8,4},{12,8},{16,12},{20,16},{24,20},{28,24},{5,1},{9,5},{13... | collective-permute-start | bytes 430088 | tf_op jit(solution)/shard_map/ppermute | solution.py:25
  91.6 65.3 %collective-permute-start.9 = (f32[3,8,32]{2,1,0:T(8,128)S(1)}, f32[3,8,32]{2,1,0:T(8,128)S(1)}, u32[]{:S(2)}, u32[]{:S(2)}) collective-permute-start(f32[3,8,32]{2,1,0:T(8,128)S(1)} %copy-done.12), channel_id=1, source_target_pairs={{4,0},{8,4},{12,8},{16,12},{20,16},{24,20},{28,24},{5,1},{9,5},{13... | collective-permute-start | bytes 9224 | tf_op jit(solution)/shard_map/ppermute | solution.py:25
  92.9 75.9 %collective-permute-start.2 = (f32[3,8,32]{2,1,0:T(8,128)}, f32[3,8,32]{2,1,0:T(8,128)S(1)}, u32[]{:S(2)}, u32[]{:S(2)}) collective-permute-start(f32[3,8,32]{2,1,0:T(8,128)} %get-tuple-element.105), channel_id=1, source_target_pairs={{0,4},{4,8},{8,12},{12,16},{16,20},{20,24},{24,28},{1,5},{5,9},{9,... | collective-permute-start | bytes 9224 | tf_op jit(solution)/shard_map/ppermute | solution.py:22
  98.1 70.6 %collective-permute-start.3 = (f32[3,8,32]{2,1,0:T(8,128)}, f32[3,8,32]{2,1,0:T(8,128)S(1)}, u32[]{:S(2)}, u32[]{:S(2)}) collective-permute-start(f32[3,8,32]{2,1,0:T(8,128)} %get-tuple-element.106), channel_id=1, source_target_pairs={{4,0},{8,4},{12,8},{16,12},{20,16},{24,20},{28,24},{5,1},{9,5},{13... | collective-permute-start | bytes 9224 | tf_op jit(solution)/shard_map/ppermute | solution.py:25
  157.6 17.1 %copy-start.1 = (f32[32,32,3,32]{3,2,1,0:T(4,128)S(1)}, f32[32,32,3,32]{3,2,1,0:T(4,128)}, u32[]{:S(2)}) copy-start(f32[32,32,3,32]{3,2,1,0:T(4,128)} %reshape.157) | copy-start | bytes 1179652
  186.3 22.9 %copy-start.6 = (f32[8,8192]{1,0:T(8,128)}, f32[8,8192]{1,0:T(8,128)S(1)}, u32[]{:S(2)}) copy-start(f32[8,8192]{1,0:T(8,128)S(1)} %multiply_add_fusion) | copy-start | bytes 786436
  (10 other events, 47.5 us)
Sparse Core Ops, SparseCore 0:
  17.8 19.0 all-gather.1
  157.0 28.2 reduce-scatter.1
where the time goes:
time: 217 us; the launch traced here: 216 us
  blocking collectives  52.8 us (24%)
  local copies, waits for them, and re-layouts  52.2 us (24%)
  matrix products  48 us (22%)
  starting transfers between devices  33.5 us (15%)
  between operations  15.5 us (7%)
  other arithmetic  9.62 us (4%)
  waiting for transfers between devices  3.15 us (1%)
    all_gather x1, blocking collectives, on_device(): all_roots = lax.all_gather(current, 'leaf', axis=0, tiled=True)  31.5 us
    ppermute x6, starting transfers between devices, padded_2(): lax.ppermute(lax.slice_in_dim(block, block.shape[dim] - width, None, axis...  25.7 us
    psum x1, blocking collectives, on_device(): gram_matrix = lax.psum(gram_part, 'leaf') / (leaf_count * points_dev)  21.4 us
    dot_general x8, matrix products, add_block(): jnp.einsum('vbs,bts->bvt', source_rows[:columns], kernel, precision=EXACT...  19.2 us
    gather x8, local copies, waits for them, and re-layouts, add_block(): source_rows = jnp.take(window, source_ids, axis=1)  15.9 us
    gather x15, local copies, waits for them, and re-layouts, take_rows(): gathered.append(padded[np.arange(count_nodes) + shift_by + pad_width])  15.6 us
    dot_general x8, matrix products, add_block(): jnp.einsum('qs,qhg->hsg', selection_mask, contribution, precision=EXACT_A...  10.5 us
    dot_general x5, matrix products, couple_level(): jnp.einsum('navr,nras->nvs', sources, blocks, precision=EXACT_ARITHMETIC)  7.84 us
  transfers between devices with their start and end apart: 14, of which 1 were waited for; matrix products, arithmetic and copies ran while one was open for 48% of the time, Pallas kernels for 0%

commit v1 on v0

--- a/solution.py
+++ b/solution.py
@@ -12,6 +12,27 @@
 LENGTH = 0.35
 EVEN_OFFSETS = (-2, 2, 3)
 ODD_OFFSETS = (-3, -2, 2)
+
+
+def collect(value, axis, dim):
+    length, index, span = (lax.axis_size(axis), lax.axis_index(axis), value.shape[dim])
+    upward = [(i, (i + 1) % length) for i in range(length)]
+    left = [(i, (i - 1) % length) for i in range(length)]
+    whole = jnp.zeros((*value.shape[:dim], length * span, *value.shape[dim + 1 :]), value.dtype)
+    whole = lax.dynamic_update_slice_in_dim(whole, value, index * span, axis=dim)
+    from_left = from_right = value
+    half = length // 2
+    for step in range(1, half + 1):
+        from_left = lax.ppermute(from_left, axis, upward)
+        whole = lax.dynamic_update_slice_in_dim(
+            whole, from_left, (index - step) % length * span, axis=dim
+        )
+        if step < length - half:
+            from_right = lax.ppermute(from_right, axis, left)
+            whole = lax.dynamic_update_slice_in_dim(
+                whole, from_right, (index + step) % length * span, axis=dim
+            )
+    return whole
 
 
 def padded_2(block, sides, width):
@@ -200,7 +221,7 @@
         nodes_here //= 2
     top_levels = top_ops.shape[0]
     top_fields = []
-    all_roots = lax.all_gather(current, "leaf", axis=0, tiled=True)
+    all_roots = collect(current, "leaf", 0)
     for height in range(top_levels):
         padded_top = jnp.pad(all_roots, ((3, 3), (0, 0), (0, 0)))
         node_id = device // (1 << height)

time: 217 us -> 306 us (1.41)
  other arithmetic: 9.62 us -> 43.8 us
  waiting for transfers between devices: 3.15 us -> 35.1 us
  blocking collectives: 52.8 us -> 21.4 us
  local copies, waits for them, and re-layouts: 52.2 us -> 76.5 us
  starting transfers between devices: 33.5 us -> 49.6 us
  matrix products: 48 us -> 60.7 us
    all_gather x1 -> x0, blocking collectives: 31.5 us -> none  [on_device(): all_roots = lax.all_gather(current, 'leaf', axis=0, tiled=True)]
    reduce_scatter x1, waiting for transfers between devices: 3.09 us -> 21.8 us  [on_device(): lax.psum_scatter(partial_sum, 'vec', scatter_dimension=0, tiled=True)]
    ppermute x0 -> x7, starting transfers between devices: none -> 18.7 us  [the longest x4 12.2 us: collect(): from_left = lax.ppermute(from_left, axis, upward)]
    and x8, other arithmetic: 0.13 us -> 10.3 us  [add_block(): target_pts = jnp.take(local_coords, target_ids, axis=1)]
    select_n x16, other arithmetic: 0.76 us -> 10.8 us  [add_block(): source_rows = jnp.take(window, source_ids, axis=1)]
    ppermute x0 -> x7, waiting for transfers between devices: none -> 8.23 us  [the longest x3 4.85 us: collect(): from_right = lax.ppermute(from_right, axis, left)]
    gather x8, local copies, waits for them, and re-layouts: 4.59 us -> 11.8 us  [add_block(): target_pts = jnp.take(local_coords, target_ids, axis=1)]
    mul x8, local copies, waits for them, and re-layouts: 0.08 us -> 5.58 us  [add_block(): (target_ids[:, None] == jnp.arange(leaves_dev)[None, :]).astype(jnp.float32)]
  transfers between devices with their start and end apart: 14 -> 21, of which waited for: 1 -> 6; matrix products, arithmetic and copies ran while one was open for 48% -> 22% of each run, Pallas kernels for 0% -> 0%
where the time goes in v1:
time: 306 us; the launch traced here: 303 us
  local copies, waits for them, and re-layouts  76.5 us (25%)
  matrix products  60.7 us (20%)
  starting transfers between devices  49.6 us (16%)
  other arithmetic  43.8 us (14%)
  waiting for transfers between devices  35.1 us (11%)
  blocking collectives  21.4 us (7%)
  between operations  15.6 us (5%)
    ppermute x6, starting transfers between devices, padded_2(): lax.ppermute(lax.slice_in_dim(block, block.shape[dim] - width, None, axis...  22.9 us
    reduce_scatter x1, waiting for transfers between devices, on_device(): lax.psum_scatter(partial_sum, 'vec', scatter_dimension=0, tiled=True)  21.8 us
    psum x1, blocking collectives, on_device(): gram_matrix = lax.psum(gram_part, 'leaf') / (leaf_count * points_dev)  21.4 us
    dot_general x8, matrix products, add_block(): jnp.einsum('vbs,bts->bvt', source_rows[:columns], kernel, precision=EXACT...  19.2 us
    gather x15, local copies, waits for them, and re-layouts, take_rows(): gathered.append(padded[np.arange(count_nodes) + shift_by + pad_width])  17.1 us
    dot_general x8, matrix products, add_block(): jnp.einsum('qs,qhg->hsg', selection_mask, contribution, precision=EXACT_A...  15.9 us
    gather x8, local copies, waits for them, and re-layouts, add_block(): source_rows = jnp.take(window, source_ids, axis=1)  15.9 us
    ppermute x4, starting transfers between devices, collect(): from_left = lax.ppermute(from_left, axis, upward)  12.2 us
  transfers between devices with their start and end apart: 21, of which 6 were waited for; matrix products, arithmetic and copies ran while one was open for 22% of the time, Pallas kernels for 0%

profile of v1, /device:TPU:0, one launch (start us, length us, event | category | flops | bytes accessed | tf_op | source)
XLA Modules:
  0.0 303.4 jit_solution(16750920427987566096)
XLA Ops:
  7.2 2.3 fusion.55
  12.1 3.0 collective-permute-start.12
  15.0 3.0 %collective-permute-start.13 = (f32[1,8,32]{2,1,0:T(8,128)}, f32[1,8,32]{2,1,0:T(8,128)}, u32[]{:S(2)}, u32[]{:S(2)}) collective-permute-start(f32[1,8,32]{2,1,0:T(8,128)} %get-tuple-element.88), channel_id=1, source_target_pairs={{0,28},{4,0},{8,4},{12,8},{16,12},{20,16},{24,20},{28,24},{1,29},{... | collective-permute-start | bytes 3080 | tf_op jit(solution)/shard_map/ppermute | solution.py:31
  21.9 4.7 %collective-permute-start.8 = (f32[3,8,32]{2,1,0:T(8,128)}, f32[3,8,32]{2,1,0:T(8,128)S(1)}, u32[]{:S(2)}, u32[]{:S(2)}) collective-permute-start(f32[3,8,32]{2,1,0:T(8,128)} %get-tuple-element.108), channel_id=1, source_target_pairs={{0,4},{4,8},{8,12},{12,16},{16,20},{20,24},{24,28},{1,5},{5,9},{9,... | collective-permute-start | bytes 9224 | tf_op jit(solution)/shard_map/ppermute | solution.py:43
  42.4 3.2 %reshape.157 = f32[32,32,3,32]{3,2,1,0:T(4,128)} reshape(f32[32,32,96]{2,1,0:T(8,128)} %slice.211) | data formatting | bytes 786432 | tf_op jit(solution)/shard_map/reshape | solution.py:73
  52.5 4.9 %collective-permute-start.6 = (f32[3,8,32]{2,1,0:T(8,128)S(1)}, f32[3,8,32]{2,1,0:T(8,128)S(1)}, u32[]{:S(2)}, u32[]{:S(2)}) collective-permute-start(f32[3,8,32]{2,1,0:T(8,128)S(1)} %copy-done.23), channel_id=1, source_target_pairs={{0,4},{4,8},{8,12},{12,16},{16,20},{20,24},{24,28},{1,5},{5,9},{9,... | collective-permute-start | bytes 9224 | tf_op jit(solution)/shard_map/ppermute | solution.py:43
  59.4 3.6 %collective-permute-start.14 = (f32[1,8,32]{2,1,0:T(8,128)}, f32[1,8,32]{2,1,0:T(8,128)S(1)}, u32[]{:S(2)}, u32[]{:S(2)}) collective-permute-start(f32[1,8,32]{2,1,0:T(8,128)} %collective-permute-done.12), channel_id=1, source_target_pairs={{0,4},{4,8},{8,12},{12,16},{16,20},{20,24},{24,28},{28,0},{1,5},{5... | collective-permute-start | bytes 3080 | tf_op jit(solution)/shard_map/ppermute | solution.py:26
  67.6 2.2 collective-permute-start.15
  69.7 2.5 collective-permute-done.15
  72.3 2.9 collective-permute-start.16
  75.2 3.4 %collective-permute-done.16 = f32[1,8,32]{2,1,0:T(8,128)S(1)} collective-permute-done((f32[1,8,32]{2,1,0:T(8,128)S(1)}, f32[1,8,32]{2,1,0:T(8,128)S(1)}, u32[]{:S(2)}, u32[]{:S(2)}) %collective-permute-start.16) | collective-permute-done | bytes 1056 | tf_op jit(solution)/shard_map/ppermute | solution.py:26
  79.9 2.3 collective-permute-done.17
  82.2 3.6 %collective-permute-start.4 = (f32[3,8,32]{2,1,0:T(8,128)}, f32[3,8,32]{2,1,0:T(8,128)}, u32[]{:S(2)}, u32[]{:S(2)}) collective-permute-start(f32[3,8,32]{2,1,0:T(8,128)} %get-tuple-element.102), channel_id=1, source_target_pairs={{0,4},{4,8},{8,12},{12,16},{16,20},{20,24},{24,28},{1,5},{5,9},{9,... | collective-permute-start | bytes 9224 | tf_op jit(solution)/shard_map/ppermute | solution.py:43
  87.7 4.5 %collective-permute-start.2 = (f32[3,8,32]{2,1,0:T(8,128)}, f32[3,8,32]{2,1,0:T(8,128)S(1)}, u32[]{:S(2)}, u32[]{:S(2)}) collective-permute-start(f32[3,8,32]{2,1,0:T(8,128)} %get-tuple-element.100), channel_id=1, source_target_pairs={{0,4},{4,8},{8,12},{12,16},{16,20},{20,24},{24,28},{1,5},{5,9},{9,... | collective-permute-start | bytes 9224 | tf_op jit(solution)/shard_map/ppermute | solution.py:43
  94.3 2.7 collective-permute-start.18
  109.6 2.4 convolution_bitcast_fusion.2
  112.0 4.7 %fusion.46 = f32[32,8,32]{2,1,0:T(8,128)} fusion(f32[32,32,3,32]{3,2,1,0:T(4,128)} %reshape.157, f32[32,1,8,32]{3,2,0,1:T(8,128)} %bitcast.181, f32[32,1,8,32]{3,2,0,1:T(8,128)} %bitcast.180, f32[32,1,8,32]{3,2,0,1:T(8,128)} %bitcast.182), kind=kOutput, calls=%fused_computation.89 | convolution fusion | flops 9486336 | bytes 524288 | tf_op jit(solution)/shard_map/navr,nras->nvs/dot_general | solution.py:74
  129.8 3.3 %collective-permute-start = (f32[35,1024]{1,0:T(8,128)S(1)}, f32[35,1024]{1,0:T(8,128)S(1)}, u32[]{:S(2)}, u32[]{:S(2)}) collective-permute-start(f32[35,1024]{1,0:T(8,128)S(1)} %get-tuple-element.98), channel_id=1, source_target_pairs={{0,4},{4,8},{8,12},{12,16},{16,20},{20,24},{24,28},{1,5},{5,9},{9,... | collective-permute-start | bytes 430088 | tf_op jit(solution)/shard_map/ppermute | solution.py:43
  135.9 4.4 %collective-permute-done.1 = f32[35,1024]{1,0:T(8,128)S(1)} collective-permute-done((f32[35,1024]{1,0:T(8,128)S(1)}, f32[35,1024]{1,0:T(8,128)S(1)}, u32[]{:S(2)}, u32[]{:S(2)}) %collective-permute-start.1) | collective-permute-done | bytes 143392 | tf_op jit(solution)/shard_map/ppermute | solution.py:46
  142.7 101.5 %while.11 = (s32[]{:T(128)}, f32[32,32,256]{2,1,0:T(8,128)S(1)}, s32[8,5]{1,0:T(8,128)}, f32[35,40,256]{2,0,1:T(8,128)}, s32[8,5]{1,0:T(8,128)}, /*index=5*/f32[...) while((s32[]{:T(128)}, f32[32,32,256]{2,1,0:T(8,128)S(1)}, s32[8,5]{1,0:T(8,128)}, ...), condition=%wide.region_1.2_spmd.clone, body=%wide.region_0.1_spmd.clone.sunk | while | flops 146720672 | bytes 3547571 | solution.py:167
  150.3 2.4 fusion.197
  153.4 2.0 fusion.199
  163.0 2.4 fusion.197
  175.6 2.4 fusion.197
  188.3 2.4 fusion.197
  201.0 2.4 fusion.197
  213.7 2.4 fusion.197
  226.4 2.4 fusion.197
  229.5 2.0 fusion.199
  239.1 2.4 fusion.197
  250.8 21.8 %reduce-scatter.2.cloned.1.call-done = f32[8,8192]{1,0:T(8,128)} async-done(((f32[32,8192]{1,0:T(8,128)}), f32[8,8192]{1,0:T(8,128)}) %reduce-scatter.2.cloned.1.call-update) | async-done | bytes 262160 | tf_op jit(solution)/shard_map/reduce_scatter | solution.py:201
  274.5 21.4 %psum.7 = f32[32,8]{0,1:T(8,128)S(1)} all-reduce(f32[32,8]{0,1:T(8,128)S(1)} %convolution_bitcast_fusion.5), channel_id=1, replica_groups=mesh['leaf'=8,'vec'=4] {'leaf'}, use_global_device_ids=true, to_apply=%region_3.4 | all-reduce | flops 256 | bytes 2048 | tf_op jit(solution)/shard_map/psum | solution.py:247
  (360 shorter events, 156.9 us)
Async XLA Ops:
  7.2 120.3 %all-gather.2.cloned.1.call-start = ((), (), s32[]{:S(2)}) async-start(), calls=%async_computation.1 | async-start | bytes 1310720 | tf_op jit(solution)/shard_map/all_gather | solution.py:180
  10.7 19.7 %copy-start.7 = (f32[8,8,32]{2,1,0:T(8,128)}, f32[8,8,32]{2,1,0:T(8,128)S(1)}, u32[]{:S(2)}) copy-start(f32[8,8,32]{2,1,0:T(8,128)S(1)} %slice_add_fusion.1) | copy-start | bytes 24580
  12.1 38.5 %collective-permute-start.12 = (f32[1,8,32]{2,1,0:T(8,128)}, f32[1,8,32]{2,1,0:T(8,128)}, u32[]{:S(2)}, u32[]{:S(2)}) collective-permute-start(f32[1,8,32]{2,1,0:T(8,128)} %get-tuple-element.88), channel_id=1, source_target_pairs={{0,4},{4,8},{8,12},{12,16},{16,20},{20,24},{24,28},{28,0},{1,5},{5... | collective-permute-start | bytes 3080 | tf_op jit(solution)/shard_map/ppermute | solution.py:26
  15.0 37.5 %collective-permute-start.13 = (f32[1,8,32]{2,1,0:T(8,128)}, f32[1,8,32]{2,1,0:T(8,128)}, u32[]{:S(2)}, u32[]{:S(2)}) collective-permute-start(f32[1,8,32]{2,1,0:T(8,128)} %get-tuple-element.88), channel_id=1, source_target_pairs={{0,28},{4,0},{8,4},{12,8},{16,12},{20,16},{24,20},{28,24},{1,29},{... | collective-permute-start | bytes 3080 | tf_op jit(solution)/shard_map/ppermute | solution.py:31
  18.1 40.0 %collective-permute-start.10 = (f32[2,8,32]{2,1,0:T(8,128)S(1)}, f32[2,8,32]{2,1,0:T(8,128)}, u32[]{:S(2)}, u32[]{:S(2)}) collective-permute-start(f32[2,8,32]{2,1,0:T(8,128)S(1)} %slice_add_fusion.3), channel_id=1, source_target_pairs={{0,4},{4,8},{8,12},{12,16},{16,20},{20,24},{24,28},{1,5},{5,9},{9,... | collective-permute-start | bytes 6152 | tf_op jit(solution)/shard_map/ppermute | solution.py:43
  19.9 39.4 %collective-permute-start.11 = (f32[2,8,32]{2,1,0:T(8,128)S(1)}, f32[2,8,32]{2,1,0:T(8,128)}, u32[]{:S(2)}, u32[]{:S(2)}) collective-permute-start(f32[2,8,32]{2,1,0:T(8,128)S(1)} %slice_add_fusion.3), channel_id=1, source_target_pairs={{4,0},{8,4},{12,8},{16,12},{20,16},{24,20},{28,24},{5,1},{9,5},{13... | collective-permute-start | bytes 6152 | tf_op jit(solution)/shard_map/ppermute | solution.py:46
  21.3 251.3 %reduce-scatter.2.cloned.1.call-start = ((), (), s32[]{:S(2)}) async-start(), calls=%async_computation.2 | async-start | bytes 1310720 | tf_op jit(solution)/shard_map/reduce_scatter | solution.py:201
  21.9 71.0 %collective-permute-start.8 = (f32[3,8,32]{2,1,0:T(8,128)}, f32[3,8,32]{2,1,0:T(8,128)S(1)}, u32[]{:S(2)}, u32[]{:S(2)}) collective-permute-start(f32[3,8,32]{2,1,0:T(8,128)} %get-tuple-element.108), channel_id=1, source_target_pairs={{0,4},{4,8},{8,12},{12,16},{16,20},{20,24},{24,28},{1,5},{5,9},{9,... | collective-permute-start | bytes 9224 | tf_op jit(solution)/shard_map/ppermute | solution.py:43
  26.7 10.4 %copy-start.28 = (s32[16]{0:T(128)S(1)}, s32[16]{0:T(128)}, u32[]{:S(2)}) copy-start(s32[16]{0:T(128)} %constant.253) | copy-start | bytes 196
  26.8 10.9 %copy-start.26 = (s32[32]{0:T(128)S(1)}, s32[32]{0:T(128)}, u32[]{:S(2)}) copy-start(s32[32]{0:T(128)} %constant.250) | copy-start | bytes 388
  26.8 10.9 %copy-start.27 = (s32[32]{0:T(128)S(1)}, s32[32]{0:T(128)}, u32[]{:S(2)}) copy-start(s32[32]{0:T(128)} %constant.251) | copy-start | bytes 388
  26.8 11.5 %copy-start.24 = (s32[160]{0:T(256)S(1)}, s32[160]{0:T(256)}, u32[]{:S(2)}) copy-start(s32[160]{0:T(256)} %param.46) | copy-start | bytes 1924
  26.8 11.5 %copy-start.25 = (s32[160]{0:T(256)S(1)}, s32[160]{0:T(256)}, u32[]{:S(2)}) copy-start(s32[160]{0:T(256)} %param.45) | copy-start | bytes 1924
  45.6 12.5 %copy-start.22 = (f32[3,8,32]{2,1,0:T(8,128)S(1)}, f32[3,8,32]{2,1,0:T(8,128)}, u32[]{:S(2)}) copy-start(f32[3,8,32]{2,1,0:T(8,128)} %get-tuple-element.107) | copy-start | bytes 9220
  45.6 46.6 %copy-start.8 = (f32[8,8,32]{2,1,0:T(8,128)S(1)}, f32[8,8,32]{2,1,0:T(8,128)}, u32[]{:S(2)}) copy-start(f32[8,8,32]{2,1,0:T(8,128)} %copy-done.7) | copy-start | bytes 24580
  50.5 43.8 %collective-permute-start.9 = (f32[3,8,32]{2,1,0:T(8,128)}, f32[3,8,32]{2,1,0:T(8,128)S(1)}, u32[]{:S(2)}, u32[]{:S(2)}) collective-permute-start(f32[3,8,32]{2,1,0:T(8,128)} %get-tuple-element.109), channel_id=1, source_target_pairs={{4,0},{8,4},{12,8},{16,12},{20,16},{24,20},{28,24},{5,1},{9,5},{13... | collective-permute-start | bytes 9224 | tf_op jit(solution)/shard_map/ppermute | solution.py:46
  52.5 33.3 %collective-permute-start.6 = (f32[3,8,32]{2,1,0:T(8,128)S(1)}, f32[3,8,32]{2,1,0:T(8,128)S(1)}, u32[]{:S(2)}, u32[]{:S(2)}) collective-permute-start(f32[3,8,32]{2,1,0:T(8,128)S(1)} %copy-done.23), channel_id=1, source_target_pairs={{0,4},{4,8},{8,12},{12,16},{16,20},{20,24},{24,28},{1,5},{5,9},{9,... | collective-permute-start | bytes 9224 | tf_op jit(solution)/shard_map/ppermute | solution.py:43
  58.1 29.0 %collective-permute-start.7 = (f32[3,8,32]{2,1,0:T(8,128)S(1)}, f32[3,8,32]{2,1,0:T(8,128)S(1)}, u32[]{:S(2)}, u32[]{:S(2)}) collective-permute-start(f32[3,8,32]{2,1,0:T(8,128)S(1)} %copy-done.22), channel_id=1, source_target_pairs={{4,0},{8,4},{12,8},{16,12},{20,16},{24,20},{28,24},{5,1},{9,5},{13... | collective-permute-start | bytes 9224 | tf_op jit(solution)/shard_map/ppermute | solution.py:46
  59.4 8.2 %collective-permute-start.14 = (f32[1,8,32]{2,1,0:T(8,128)}, f32[1,8,32]{2,1,0:T(8,128)S(1)}, u32[]{:S(2)}, u32[]{:S(2)}) collective-permute-start(f32[1,8,32]{2,1,0:T(8,128)} %collective-permute-done.12), channel_id=1, source_target_pairs={{0,4},{4,8},{8,12},{12,16},{16,20},{20,24},{24,28},{28,0},{1,5},{5... | collective-permute-start | bytes 3080 | tf_op jit(solution)/shard_map/ppermute | solution.py:26
  67.6 4.7 %collective-permute-start.15 = (f32[1,8,32]{2,1,0:T(8,128)}, f32[1,8,32]{2,1,0:T(8,128)S(1)}, u32[]{:S(2)}, u32[]{:S(2)}) collective-permute-start(f32[1,8,32]{2,1,0:T(8,128)} %collective-permute-done.13), channel_id=1, source_target_pairs={{0,28},{4,0},{8,4},{12,8},{16,12},{20,16},{24,20},{28,24},{1,29},{... | collective-permute-start | bytes 3080 | tf_op jit(solution)/shard_map/ppermute | solution.py:31
  72.3 6.3 %collective-permute-start.16 = (f32[1,8,32]{2,1,0:T(8,128)S(1)}, f32[1,8,32]{2,1,0:T(8,128)S(1)}, u32[]{:S(2)}, u32[]{:S(2)}) collective-permute-start(f32[1,8,32]{2,1,0:T(8,128)S(1)} %collective-permute-done.14), channel_id=1, source_target_pairs={{0,4},{4,8},{8,12},{12,16},{16,20},{20,24},{24,28},{28,0},{1,5},{5... | collective-permute-start | bytes 3080 | tf_op jit(solution)/shard_map/ppermute | solution.py:26
  78.6 3.6 %collective-permute-start.17 = (f32[1,8,32]{2,1,0:T(8,128)S(1)}, f32[1,8,32]{2,1,0:T(8,128)S(1)}, u32[]{:S(2)}, u32[]{:S(2)}) collective-permute-start(f32[1,8,32]{2,1,0:T(8,128)S(1)} %collective-permute-done.15), channel_id=1, source_target_pairs={{0,28},{4,0},{8,4},{12,8},{16,12},{20,16},{24,20},{28,24},{1,29},{... | collective-permute-start | bytes 3080 | tf_op jit(solution)/shard_map/ppermute | solution.py:31
  82.2 35.5 %collective-permute-start.4 = (f32[3,8,32]{2,1,0:T(8,128)}, f32[3,8,32]{2,1,0:T(8,128)}, u32[]{:S(2)}, u32[]{:S(2)}) collective-permute-start(f32[3,8,32]{2,1,0:T(8,128)} %get-tuple-element.102), channel_id=1, source_target_pairs={{0,4},{4,8},{8,12},{12,16},{16,20},{20,24},{24,28},{1,5},{5,9},{9,... | collective-permute-start | bytes 9224 | tf_op jit(solution)/shard_map/ppermute | solution.py:43
  85.8 31.9 %collective-permute-start.5 = (f32[3,8,32]{2,1,0:T(8,128)}, f32[3,8,32]{2,1,0:T(8,128)}, u32[]{:S(2)}, u32[]{:S(2)}) collective-permute-start(f32[3,8,32]{2,1,0:T(8,128)} %get-tuple-element.103), channel_id=1, source_target_pairs={{4,0},{8,4},{12,8},{16,12},{20,16},{24,20},{28,24},{5,1},{9,5},{13... | collective-permute-start | bytes 9224 | tf_op jit(solution)/shard_map/ppermute | solution.py:46
  87.7 16.4 %collective-permute-start.2 = (f32[3,8,32]{2,1,0:T(8,128)}, f32[3,8,32]{2,1,0:T(8,128)S(1)}, u32[]{:S(2)}, u32[]{:S(2)}) collective-permute-start(f32[3,8,32]{2,1,0:T(8,128)} %get-tuple-element.100), channel_id=1, source_target_pairs={{0,4},{4,8},{8,12},{12,16},{16,20},{20,24},{24,28},{1,5},{5,9},{9,... | collective-permute-start | bytes 9224 | tf_op jit(solution)/shard_map/ppermute | solution.py:43
  93.0 11.7 %collective-permute-start.3 = (f32[3,8,32]{2,1,0:T(8,128)}, f32[3,8,32]{2,1,0:T(8,128)}, u32[]{:S(2)}, u32[]{:S(2)}) collective-permute-start(f32[3,8,32]{2,1,0:T(8,128)} %get-tuple-element.101), channel_id=1, source_target_pairs={{4,0},{8,4},{12,8},{16,12},{20,16},{24,20},{28,24},{5,1},{9,5},{13... | collective-permute-start | bytes 9224 | tf_op jit(solution)/shard_map/ppermute | solution.py:46
  94.3 28.1 %collective-permute-start.18 = (f32[1,8,32]{2,1,0:T(8,128)S(1)}, f32[1,8,32]{2,1,0:T(8,128)S(1)}, u32[]{:S(2)}, u32[]{:S(2)}) collective-permute-start(f32[1,8,32]{2,1,0:T(8,128)S(1)} %collective-permute-done.16), channel_id=1, source_target_pairs={{0,4},{4,8},{8,12},{12,16},{16,20},{20,24},{24,28},{28,0},{1,5},{5... | collective-permute-start | bytes 3080 | tf_op jit(solution)/shard_map/ppermute | solution.py:26
  129.8 6.1 %collective-permute-start = (f32[35,1024]{1,0:T(8,128)S(1)}, f32[35,1024]{1,0:T(8,128)S(1)}, u32[]{:S(2)}, u32[]{:S(2)}) collective-permute-start(f32[35,1024]{1,0:T(8,128)S(1)} %get-tuple-element.98), channel_id=1, source_target_pairs={{0,4},{4,8},{8,12},{12,16},{16,20},{20,24},{24,28},{1,5},{5,9},{9,... | collective-permute-start | bytes 430088 | tf_op jit(solution)/shard_map/ppermute | solution.py:43
  133.1 7.2 %collective-permute-start.1 = (f32[35,1024]{1,0:T(8,128)S(1)}, f32[35,1024]{1,0:T(8,128)S(1)}, u32[]{:S(2)}, u32[]{:S(2)}) collective-permute-start(f32[35,1024]{1,0:T(8,128)S(1)} %get-tuple-element.99), channel_id=1, source_target_pairs={{4,0},{8,4},{12,8},{16,12},{20,16},{24,20},{28,24},{5,1},{9,5},{13... | collective-permute-start | bytes 430088 | tf_op jit(solution)/shard_map/ppermute | solution.py:46
  249.1 23.5 %copy-start.3 = (f32[8,8192]{1,0:T(8,128)S(1)}, f32[8,8192]{1,0:T(8,128)}, u32[]{:S(2)}) copy-start(f32[8,8192]{1,0:T(8,128)} %param.40) | copy-start | bytes 786436
  250.1 23.5 %copy-start.1 = (f32[32,8192]{1,0:T(8,128)S(1)}, f32[32,8192]{1,0:T(8,128)}, u32[]{:S(2)}) copy-start(f32[32,8192]{1,0:T(8,128)} %all-gather.2.cloned.1.call-done) | copy-start | bytes 3145732
  273.6 22.9 %copy-start.4 = (f32[8,8192]{1,0:T(8,128)}, f32[8,8192]{1,0:T(8,128)S(1)}, u32[]{:S(2)}) copy-start(f32[8,8192]{1,0:T(8,128)S(1)} %multiply_add_fusion) | copy-start | bytes 786436
  (28 other events, 153.2 us)
Sparse Core Ops, SparseCore 0:
  21.4 18.9 all-gather.1
  246.1 26.5 reduce-scatter.1
